TPU v7x, 32 devices: a whole 2x2x4 slice. The times are simulated.
32 devices in a mesh: blk: 32 (over z, y, x, core), feat: 1.
Axes of the slice: x: 2, y: 2, z: 4, core: 2. Of those that a mesh axis runs over, the one named last changes fastest.
Arguments:
- activations: bfloat16 [5120, 4096], P('blk', 'feat'), may hold values from -6 to 6
- live_rows: int32 [32], replicated, may hold values from 1 to 160, as said below
- encoder_weight: bfloat16 [4096, 32768], P('feat', 'blk'), may hold values from -0.09375 to 0.09375
- encoder_bias: float32 [32768], P('blk'), may hold values from -3 to 3
- decoder_weight: bfloat16 [4, 1024, 32768], P(None, 'feat', 'blk'), may hold values from -0.09375 to 0.09375
- decoder_bias: float32 [32768], P('blk'), may hold values from -3 to 3
- targets: bfloat16 [640, 32768], P('feat', 'blk'), may hold values from -6 to 6
Outputs:
- reconstruction: float32 [640, 32768], P('feat', 'blk')
- decoder_grad: float32 [4, 1024, 32768], P(None, 'feat', 'blk')
Inputs may be any that keep to these rules, and one draw needn't show every extreme that they name: `live_rows`: live rows of a block of 160 slots are its first ones; some block is full.
All inputs are finite; a program needn't handle non-finite values.
Results may differ from a plain program's by a relative error of at most 0.015.
Values may be sent and summed in bfloat16 or wider, within the bound.
A program may use at most 128 MiB of HBM per device.

v0:
```python
import functools

import jax
import jax.numpy as jnp
from jax import lax
from jax.experimental import pallas as pl
from jax.experimental.pallas import tpu as pltpu
from jax.sharding import PartitionSpec as P

G = 8
TILE = 16
MESH = pl.DeviceIdType.MESH


def cuts(rows, parts):
    if rows % 16 or rows // 16 < len(parts):
        return [(0, rows)]
    tiles, total, edges = rows // 16, sum(parts), [0]
    for k in range(1, len(parts)):
        edges.append(max(edges[-1] + 1, tiles * sum(parts[:k]) // total))
    edges.append(tiles)
    return [(16 * a, 16 * (b - a)) for a, b in zip(edges[:-1], edges[1:])]


def pieces_of(early, rest):
    first = [(0, *cut) for cut in cuts(early, (1,))]
    if rest:
        late = [(1, *cut) for cut in cuts(early, (1,))]
        return first + late + [(2, *cut) for cut in cuts(rest, (1,))]
    return first + [(1, *cut) for cut in cuts(early, (1, 1))]


def step(count):
    return jnp.clip(count, 0, 1)


def tile_of(first_live, second_live, tiles, k):
    first = first_live + TILE - 1 >> 4
    second = second_live + TILE - 1 >> 4
    late = 1 - step(first - k)
    inside = jnp.minimum(k - late * first, tiles - 1)
    live = first_live + late * (second_live - first_live) - TILE * inside
    return late, inside, step(first + second - k) * live


def slot_of(late, inside, sent):
    over = step(inside - sent + 1)
    return (late + over - 2 * late * over) * sent + inside + over * (2 * sent - 1 - 2 * inside)


def gather_kernel(
    sent,
    early,
    pieces,
    act_hbm,
    live_hbm,
    enc_hbm,
    bias_hbm,
    dec_hbm,
    dec_bias_hbm,
    targets_hbm,
    codes,
    residual,
    summed,
    acts_home,
    acts_away,
    spill,
    packed,
    enc,
    dec,
    part,
    targets,
    packed_targets,
    keep,
    live_ref,
    bias_ref,
    dec_bias_ref,
    load_sem,
    s1_send,
    s1_recv,
    s2_send,
    s2_recv,
    s3_send,
    s3_recv,
    t1_send,
    t1_recv,
    t2_send,
    t2_recv,
    t3_send,
    t3_recv,
):
    position = lax.axis_index("blk")
    share = lax.axis_index("feat")
    base = position // 4 * 4
    me = position % 4
    core = me % 2
    home = me - core
    away = 2 - home
    chip = home // 2
    other = 1 - chip
    twin = home + 1 - core
    peer = away + core
    peer_twin = away + 1 - core
    on_chip = (base + twin, share)
    across = (base + peer, share)

    block_tiles = act_hbm.shape[0]
    spare = block_tiles - sent
    act_cuts = [(0, sent - spare)] + [(sent - spare, spare)] * (spare > 0)
    total = codes.shape[1]
    rest = total - 2 * early
    width = enc.shape[1]
    column_tile = min(256, width)
    columns = width // column_tile

    def own_tiles(at_core, start, count):
        return pl.ds(at_core * block_tiles + start, count)

    load_act = pltpu.make_async_copy(
        act_hbm, acts_home.at[own_tiles(core, 0, block_tiles)], load_sem.at[0]
    )
    load_enc = pltpu.make_async_copy(enc_hbm, enc, load_sem.at[1])
    load_dec = pltpu.make_async_copy(dec_hbm, dec, load_sem.at[2])
    load_targets = pltpu.make_async_copy(targets_hbm, targets, load_sem.at[3])
    load_live = pltpu.make_async_copy(live_hbm, live_ref, load_sem.at[4])
    load_bias = pltpu.make_async_copy(bias_hbm, bias_ref, load_sem.at[5])
    load_dec_bias = pltpu.make_async_copy(dec_bias_hbm, dec_bias_ref, load_sem.at[6])
    load_live.start()
    load_bias.start()
    load_act.start()
    load_enc.start()
    load_dec_bias.start()

    barrier = pltpu.get_barrier_semaphore()
    for neighbour in (on_chip, across):
        pl.semaphore_signal(barrier, inc=1, device_id=neighbour, device_id_type=MESH)
    pl.semaphore_wait(barrier, 2)

    def remote(src, dst, send, recv, to):
        return pltpu.make_async_remote_copy(
            src_ref=src,
            dst_ref=dst,
            send_sem=send,
            recv_sem=recv,
            device_id=to,
            device_id_type=MESH,
        )

    def s1(at_core):
        ref = acts_home.at[own_tiles(at_core, 0, block_tiles)]
        return remote(act_hbm, ref, s1_send.at[0], s1_recv.at[0], on_chip)

    def s2(h):
        at, count = act_cuts[h]
        src = spill if h else act_hbm.at[pl.ds(at, count)]
        ref = acts_away.at[pl.ds(core * sent + at, count)]
        return remote(src, ref, s2_send.at[h], s2_recv.at[h], across)

    def s3(at_core):
        ref = acts_away.at[pl.ds(at_core * sent, sent)]
        return remote(ref, ref, s3_send.at[0], s3_recv.at[0], on_chip)

    def region(kind, of_chip, start, count):
        first = (of_chip * early, (1 - of_chip) * early, 2 * early)[kind]
        return pl.ds(pl.multiple_of(first + start, TILE), count)

    sizes = (early, early, rest)
    kinds = (0, 1, 2) if rest else (0, 1)

    def t1(f, kind):
        ref = codes.at[f, region(kind, chip, 0, sizes[kind])]
        return remote(ref, ref, t1_send.at[kind], t1_recv.at[kind], on_chip)

    def t2(f, p, of_chip):
        kind, start, count = pieces[p]
        ref = codes.at[f, region(kind, of_chip, start, count)]
        return remote(ref, ref, t2_send.at[p], t2_recv.at[p], across)

    def t3(f, p):
        kind, start, count = pieces[p]
        ref = codes.at[f, region(kind, other, start, count)]
        return remote(ref, ref, t3_send.at[p], t3_recv.at[p], on_chip)

    def send(kind):
        t1(me, kind).start()
        for p, piece in enumerate(pieces):
            if piece[0] == kind:
                t2(me, p, chip).start()

    s2(0).start()
    s1(core).start()
    load_dec.start()
    load_targets.start()

    def mark(at, live, where):
        keep[at] = (lax.broadcasted_iota(jnp.int32, (TILE, keep.shape[1]), 0) < live).astype(
            jnp.float32
        )
        packed_targets[at] = targets[where]

    def pack(acts, of_chip):
        first_live = live_ref[base + 2 * of_chip]
        second_live = live_ref[base + 2 * of_chip + 1]

        def one(k, carry):
            late, inside, live = tile_of(first_live, second_live, block_tiles, k)
            where = late * block_tiles + inside
            at = pl.ds(pl.multiple_of(of_chip * early + k * TILE, TILE), TILE)
            packed[at] = acts[slot_of(late, inside, sent) if acts is acts_away else where]
            mark(at, live, of_chip * 2 * block_tiles + where)
            return carry

        lax.fori_loop(0, early // TILE, one, 0)

    def pack_rest():
        lives = [live_ref[base + b] for b in range(4)]
        first_extra = jnp.maximum(
            (lives[0] + TILE - 1 >> 4) + (lives[1] + TILE - 1 >> 4) - early // TILE, 0
        )

        def one(k, carry):
            from_first = step(first_extra - k)
            index = early // TILE + k - (1 - from_first) * first_extra
            late0, inside0, live0 = tile_of(lives[0], lives[1], block_tiles, index)
            late1, inside1, live1 = tile_of(lives[2], lives[3], block_tiles, index)
            where0 = late0 * block_tiles + inside0
            where1 = late1 * block_tiles + inside1
            slot0 = slot_of(late0, inside0, sent)
            slot1 = slot_of(late1, inside1, sent)
            where_home = where0 + chip * (where1 - where0)
            where_away = slot1 + chip * (slot0 - slot1)
            at = pl.ds(pl.multiple_of(2 * early + k * TILE, TILE), TILE)
            mine = jnp.full((TILE, acts_home.shape[2]), from_first + chip, jnp.int32) == 1
            packed[at] = jnp.where(mine, acts_home[where_home], acts_away[where_away])
            mark(
                at,
                live1 + from_first * (live0 - live1),
                where1 + 2 * block_tiles + from_first * (where0 - where1 - 2 * block_tiles),
            )
            return carry

        lax.fori_loop(0, rest // TILE, one, 0)

    def encode(kind):
        here = region(kind, chip, 0, sizes[kind])

        def column(n, carry):
            at = pl.ds(pl.multiple_of(n * column_tile, column_tile), column_tile)
            product = jnp.dot(packed[here], enc[:, at], preferred_element_type=jnp.float32)
            value = product.astype(jnp.bfloat16).astype(jnp.float32) + bias_ref[:, at]
            codes[me, here, at] = jnp.maximum(value, 0.0).astype(jnp.bfloat16)
            return carry

        lax.fori_loop(0, columns, column, 0)

    def home_features(kind):
        here = region(kind, chip, 0, sizes[kind])

        def column(n, carry):
            at = pl.ds(pl.multiple_of(n * column_tile, column_tile), column_tile)
            first = jnp.dot(
                codes[me, here], dec[me, :, at], preferred_element_type=jnp.float32
            )
            second = jnp.dot(
                codes[twin, here], dec[twin, :, at], preferred_element_type=jnp.float32
            )
            part[here, at] = first + second
            return carry

        lax.fori_loop(0, columns, column, 0)

    def finish(p):
        kind, start, count = pieces[p]
        here = region(kind, other, start, count)

        def add(owners, span):
            def column(n, carry):
                at = pl.ds(pl.multiple_of(n * span, span), span)
                total = part[here, at]
                for f in owners:
                    total += jnp.dot(
                        codes[f, here], dec[f, :, at], preferred_element_type=jnp.float32
                    )
                part[here, at] = total
                return carry

            lax.fori_loop(0, width // span, column, 0)

        t2(peer, p, other).wait_recv()
        t3(peer, p).start()
        if p == len(pieces) - 1:
            add([peer], width)
            t3(peer_twin, p).wait_recv()
            add([peer_twin], width)
        else:
            t3(peer_twin, p).wait_recv()
            add([peer, peer_twin], column_tile)
        whole = part[here].astype(jnp.bfloat16)
        summed[here] = whole
        error = (
            whole.astype(jnp.float32)
            + dec_bias_ref[...]
            - packed_targets[here].astype(jnp.float32)
        )
        live = jnp.concatenate([keep[here]] * (width // keep.shape[1]), axis=1)
        residual[here] = jnp.where(live > 0.0, error, 0.0).astype(jnp.bfloat16)

    load_live.wait()
    load_bias.wait()
    load_dec_bias.wait()
    load_act.wait()
    s1(1 - core).wait_recv()
    twin_tiles = live_ref[base + twin] + TILE - 1 >> 4
    for i in range(spare):
        own = core * block_tiles + sent - 1 - i
        theirs = (1 - core) * block_tiles + sent + i
        spill[spare - 1 - i] = acts_home[own + step(twin_tiles - sent - i) * (theirs - own)]
    for h in range(1, len(act_cuts)):
        s2(h).start()
    load_targets.wait()
    pack(acts_home, chip)
    load_enc.wait()
    encode(0)
    send(0)
    load_dec.wait()
    t1(twin, 0).wait_recv()
    home_features(0)

    for h in range(len(act_cuts)):
        s2(h).wait_recv()
    s3(core).start()
    s3(1 - core).wait_recv()
    pack(acts_away, other)
    encode(1)
    send(1)
    if rest:
        pack_rest()
        encode(2)
        send(2)
    for kind in kinds[1:]:
        t1(twin, kind).wait_recv()
        home_features(kind)
    for p in range(len(pieces)):
        finish(p)

    s1(core).wait_send()
    for h in range(len(act_cuts)):
        s2(h).wait_send()
    s3(core).wait_send()
    for kind in kinds:
        t1(me, kind).wait_send()
    for p in range(len(pieces)):
        t2(me, p, chip).wait_send()
        t3(peer, p).wait_send()


def choice_kernel(sizes, live_ref, choice_ref):
    choice = 0
    for group in range(0, live_ref.shape[0], 4):
        counts = [live_ref[group + b] + TILE - 1 >> 4 for b in range(4)]
        most = jnp.maximum(counts[0] + counts[1], counts[2] + counts[3])
        missed = sum(
            step(sum(counts) - tiles) | step(most - 2 * sent) for tiles, sent in sizes[:-1]
        )
        choice = jnp.maximum(choice, missed)
    choice_ref[0] = choice


def gradient_kernel(
    span,
    early,
    live_ref,
    codes_ref,
    residual_ref,
    summed_ref,
    bias_ref,
    rebuilt_hbm,
    grad_hbm,
    grad,
    rebuilt,
    sem,
):
    owners, width = codes_ref.shape[0], codes_ref.shape[2]
    block_tiles = rebuilt.shape[0] // TILE // 4
    base = lax.axis_index("blk") // 4 * 4
    per = width // span

    def out(f, i):
        at = pl.ds(pl.multiple_of(i * span, span), span)
        return pltpu.make_async_copy(grad.at[f, at], grad_hbm.at[f, at], sem.at[f * per + i])

    def block(f, i):
        at = pl.ds(i * span, span)
        grad[f, at] = lax.dot_general(
            codes_ref[f, :, at],
            residual_ref[...],
            (((0,), (0,)), ((), ())),
            preferred_element_type=jnp.float32,
        )
        out(f, i).start()

    counts = [live_ref[base + b] + TILE - 1 >> 4 for b in range(4)]
    first_extra = jnp.maximum(counts[0] + counts[1] - early // TILE, 0)

    def spread(b, s):
        live = live_ref[base + b]
        chip = b // 2
        k = b % 2 * (live_ref[base + b - b % 2] + TILE - 1 >> 4) + s
        place = jnp.where(
            k < early // TILE,
            chip * (early // TILE) + k,
            early // TILE + chip * first_extra + k,
        )
        place = jnp.where(TILE * s < live, place, 0)
        value = summed_ref[pl.ds(pl.multiple_of(place * TILE, TILE), TILE)].astype(jnp.float32)
        row = TILE * s + lax.broadcasted_iota(jnp.int32, value.shape, 0)
        at = pl.ds(pl.multiple_of((b * block_tiles + s) * TILE, TILE), TILE)
        rebuilt[at] = jnp.where(row < live, value, 0.0) + bias_ref[...]

    def give(b):
        at = pl.ds(pl.multiple_of(b * block_tiles * TILE, TILE), block_tiles * TILE)
        return pltpu.make_async_copy(rebuilt.at[at], rebuilt_hbm.at[at], sem.at[owners * per + b])

    def owner(f, carry):
        for i in range(per):
            block(f, i)
            for s in range(block_tiles * i // per, block_tiles * (i + 1) // per):
                spread(f, s)
        give(f).start()
        return carry

    lax.fori_loop(0, 4, owner, 0)

    def ended(i, carry):
        out(i // per, i % per).wait()
        return carry

    lax.fori_loop(0, owners * per, ended, 0)
    for b in range(4):
        give(b).wait()


def packed_tiles(
    order,
    tiles,
    sent,
    activations,
    live_rows,
    encoder_weight,
    encoder_bias,
    decoder_weight,
    decoder_bias,
    targets,
):
    rows, depth = activations.shape
    features = encoder_weight.shape[1]
    width = decoder_weight.shape[2]
    tokens = targets.shape[0]
    total = TILE * tiles
    early = total - 2 * rows
    block_tiles = rows // TILE
    spare = block_tiles - sent
    pieces = pieces_of(early, total - 2 * early)
    lanes = min(128, width)
    any_space = pl.BlockSpec(memory_space=pl.ANY)
    stay = functools.partial(pltpu.with_memory_space_constraint, memory_space=pltpu.HBM)
    in_vmem = pl.BlockSpec(memory_space=pltpu.VMEM)
    in_smem = pl.BlockSpec(memory_space=pltpu.SMEM)
    in_hbm = pl.BlockSpec(memory_space=pltpu.HBM)
    dma = pltpu.SemaphoreType.DMA
    bf16 = jnp.bfloat16
    f32 = jnp.float32
    codes, residual, summed = pl.pallas_call(
        functools.partial(gather_kernel, sent, early, pieces),
        out_shape=(
            pltpu.VMEM((4, total, features), bf16),
            pltpu.VMEM((total, width), bf16),
            pltpu.VMEM((total, width), bf16),
        ),
        in_specs=[in_hbm] * 7,
        out_specs=(in_vmem, in_vmem, in_vmem),
        scratch_shapes=[
            pltpu.VMEM((2 * block_tiles, TILE, depth), bf16),
            pltpu.VMEM((2 * sent, TILE, depth), bf16),
            pltpu.VMEM((max(spare, 1), TILE, depth), bf16),
            pltpu.VMEM((total, depth), bf16),
            pltpu.VMEM((depth, features), bf16),
            pltpu.VMEM((4, features, width), bf16),
            pltpu.VMEM((total, width), f32),
            pltpu.VMEM((4 * block_tiles, TILE, width), bf16),
            pltpu.VMEM((total, width), bf16),
            pltpu.VMEM((total, lanes), f32),
            pltpu.SMEM(live_rows.shape, jnp.int32),
            pltpu.VMEM((1, features), f32),
            pltpu.VMEM((1, width), f32),
            dma((7,)),
            dma((1,)),
            dma((1,)),
            dma((2,)),
            dma((2,)),
            dma((1,)),
            dma((1,)),
            dma((3,)),
            dma((3,)),
            dma((len(pieces),)),
            dma((len(pieces),)),
            dma((len(pieces),)),
            dma((len(pieces),)),
        ],
        compiler_params=pltpu.CompilerParams(
            collective_id=order, has_side_effects=True, vmem_limit_bytes=44 * 1024 * 1024
        ),
        name=f"gather_codes_{tiles}_{sent}",
    )(
        activations.reshape(block_tiles, TILE, depth),
        stay(live_rows),
        encoder_weight,
        stay(encoder_bias[None, :]),
        decoder_weight,
        stay(decoder_bias[None, :]),
        targets.reshape(4 * block_tiles, TILE, width),
    )

    span = min(256, features)
    rebuilt, grad = pl.pallas_call(
        functools.partial(gradient_kernel, span, early),
        out_shape=(
            jax.ShapeDtypeStruct((tokens, width), f32),
            jax.ShapeDtypeStruct((4, features, width), f32),
        ),
        in_specs=[in_smem, in_vmem, in_vmem, in_vmem, in_vmem],
        out_specs=(any_space, any_space),
        scratch_shapes=[
            pltpu.VMEM((4, features, width), f32),
            pltpu.VMEM((tokens, width), f32),
            dma((4 * (features // span) + 4,)),
        ],
        compiler_params=pltpu.CompilerParams(vmem_limit_bytes=44 * 1024 * 1024),
        name=f"gradient_{tiles}_{sent}",
    )(live_rows, codes, residual, summed, decoder_bias[None, :])
    return rebuilt, grad


def four_owners(activations, live_rows, *operands):
    rows = activations.shape[0]
    if rows % TILE:
        return general(activations, live_rows, *operands)
    block_tiles = rows // TILE
    fewer = max(block_tiles * 9 // 10, block_tiles // 2 + 1)
    shares = ((9, fewer), (12, fewer), (12, block_tiles), (15, block_tiles), (20, block_tiles))
    sizes = sorted({(2 * block_tiles + max(1, block_tiles * k // 10), sent) for k, sent in shares})
    in_smem = pl.BlockSpec(memory_space=pltpu.SMEM)
    choice = pl.pallas_call(
        functools.partial(choice_kernel, sizes),
        out_shape=jax.ShapeDtypeStruct((1,), jnp.int32),
        in_specs=[in_smem],
        out_specs=in_smem,
        name="choice",
    )(live_rows)
    return lax.switch(
        choice[0],
        [functools.partial(packed_tiles, order, *size) for order, size in enumerate(sizes)],
        activations,
        live_rows,
        *operands,
    )


def from_partner(shard, axis, distance):
    return lax.ppermute(shard, axis, [(i, i ^ 1 << distance) for i in range(lax.axis_size(axis))])


def group_rows(block, levels, position):
    for bit in range(levels):
        other = from_partner(block, "blk", bit)
        upper = position >> bit & 1 == 1
        block = jnp.where(
            upper, jnp.concatenate([other, block], 0), jnp.concatenate([block, other], 0)
        )
    return block


def general(
    activations, live_rows, encoder_weight, encoder_bias, decoder_weight, decoder_bias, targets
):
    owners = lax.axis_size("blk") // G
    levels = owners.bit_length() - 1
    shares = lax.axis_size("feat")
    position = lax.axis_index("blk")
    share_index = lax.axis_index("feat")
    group_index = position // owners
    tok_rows = activations.shape[0]
    counts = lax.dynamic_slice_in_dim(live_rows, group_index * owners, owners)
    positions = jnp.arange(tok_rows, dtype=jnp.int32)
    live_mask = (positions[None, :] < counts[:, None]).astype(jnp.float32).reshape(-1)
    gathered = group_rows(activations, levels, position)
    per_share = encoder_weight.shape[1] // shares
    bias_share = lax.dynamic_slice_in_dim(encoder_bias, share_index * per_share, per_share)
    columns = encoder_weight
    whole = lax.psum(
        lax.dot_general(
            columns, gathered, (((0,), (1,)), ((), ())), preferred_element_type=jnp.float32
        ).astype(jnp.bfloat16),
        "feat",
    ).astype(jnp.float32)
    preact = lax.dynamic_slice_in_dim(whole, share_index * per_share, per_share, 0)
    codes_by_feature = (jax.nn.relu(preact + bias_share[:, None]) * live_mask[None, :]).astype(
        jnp.bfloat16
    )
    codes_all = group_rows(codes_by_feature, levels, position)
    decoder_rows = decoder_weight.reshape(-1, decoder_weight.shape[2])
    block_rows = gathered.shape[0] // shares
    columns = codes_all
    summed = lax.psum_scatter(
        lax.dot_general(
            columns, decoder_rows, (((0,), (0,)), ((), ())), preferred_element_type=jnp.float32
        ).astype(jnp.bfloat16),
        "feat",
        scatter_dimension=0,
        tiled=True,
    ).astype(jnp.float32)
    rebuilt = summed + decoder_bias[None, :]
    mask_block = lax.dynamic_slice_in_dim(live_mask, share_index * block_rows, block_rows)
    residual = ((rebuilt - targets.astype(jnp.float32)) * mask_block[:, None]).astype(jnp.bfloat16)
    columns = codes_all
    gradient = jnp.dot(
        columns,
        lax.all_gather(residual, "feat", axis=0, tiled=True),
        preferred_element_type=jnp.float32,
    )
    return (rebuilt, gradient.reshape(decoder_weight.shape))


def solution(mesh):
    in_specs = (
        P("blk", "feat"),
        P(),
        P("feat", "blk"),
        P("blk"),
        P(None, "feat", "blk"),
        P("blk"),
        P("feat", "blk"),
    )
    out_specs = (P("feat", "blk"), P(None, "feat", "blk"))
    fused = mesh.shape["blk"] // G == 4 and mesh.shape["feat"] == 1
    return jax.shard_map(
        four_owners if fused else general,
        mesh=mesh,
        in_specs=in_specs,
        out_specs=out_specs,
        check_vma=False,
    )
```

profile of v0, /device:TPU:0, one launch (start us, length us, event | category | flops | bytes accessed | tf_op | source)
XLA Modules:
  0.0 64.8 jit_solution(7543030295284922014)
XLA Ops:
  0.6 1.3 %choice.1 = s32[1]{0:T(128)} custom-call(s32[32]{0:T(128)} %live_ref.1), custom_call_target="tpu_custom_call" | custom-call | tf_op jit(solution)/shard_map/choice/pallas_call | solution.py:553
  2.6 62.1 %conditional.1 = ((f32[640,1024]{1,0:T(8,128)}, f32[4,1024,1024]{2,1,0:T(8,128)})) conditional(s32[]{:T(128)} %bitcast.20, (bf16[160,4096]{1,0:T(8,128)(2,1)}, f32[1024]{0:T(1024)}, f32[1024]{0:T(1024)}, bf16[640,1024]{1,0:T(8,128)(2,1)}, s32[32]{0:T(128)}, /*index=5*/bf16[4096,1024]{1,0:T(8,128)(2,1)}, ...), branch_computations={%region_0.0_spmd, %region_1.0_spmd, %region_2.0_spmd, %region_3.0_... | conditional | bytes 16960 | solution.py:560
  2.6 0.0 copy-start.1
  2.6 0.0 copy-start.6
  2.6 53.9 %gather_codes_32_9.1 = (bf16[4,512,1024]{2,1,0:T(8,128)(2,1)S(1)}, bf16[512,1024]{1,0:T(8,128)(2,1)S(1)}, bf16[512,1024]{1,0:T(8,128)(2,1)S(1)}) custom-call(bf16[10,16,4096]{2,1,0:T(8,128)(2,1)} %bitcast.22, s32[32]{0:T(128)} %get-tuple-element.80.live_hbm.live_ref, bf16[4096,1024]{1,0:T(8,128)(2,1)} %get-tuple-element.82.enc_hbm, f32[1,1024]{1,0:T(1,128)} %bitcast.42, ...), custom_call_target="tpu_custom_call" | custom-call | tf_op jit(solution)/shard_map/cond/branch_1_fun/gather_codes_32_9/pallas_call | solution.py:473
  56.6 0.0 copy-done.1
  56.6 0.0 copy-done.6
  56.6 7.8 %gradient_32_9.1 = (f32[640,1024]{1,0:T(8,128)}, f32[4,1024,1024]{2,1,0:T(8,128)}) custom-call(s32[32]{0:T(128)S(1)} %copy-done.6, bf16[4,512,1024]{2,1,0:T(8,128)(2,1)S(1)} %get-tuple-element.87.codes_ref, bf16[512,1024]{1,0:T(8,128)(2,1)S(1)} %get-tuple-element.88.residual_ref, bf16[512,1024]{1,0:T(8,128)(2,1)S(1)} %get-tuple-element.89.summed_ref, ...), custom_call_target="tpu_custom_call" | custom-call | tf_op jit(solution)/shard_map/cond/branch_1_fun/gradient_32_9/pallas_call | solution.py:525
Async XLA Ops:
  2.6 54.0 %copy-start.1 = (f32[1024]{0:T(1024)S(1)}, f32[1024]{0:T(1024)}, u32[]{:S(2)}) copy-start(f32[1024]{0:T(1024)} %get-tuple-element.85) | copy-start | bytes 12292 | tf_op jit(solution)/shard_map/cond
  2.6 54.0 %copy-start.6 = (s32[32]{0:T(128)S(1)}, s32[32]{0:T(128)}, u32[]{:S(2)}) copy-start(s32[32]{0:T(128)} %get-tuple-element.80.live_hbm.live_ref) | copy-start | bytes 388 | tf_op jit(solution)/shard_map/cond
where the time goes:
time: 64.1 us; the launch traced here: 64.8 us
  Pallas kernels  63 us (98%)
  between operations  1.47 us (2%)
    pallas_call x1, Pallas kernels, packed_tiles(): pl.pallas_call(functools.partial(gather_kernel, sent, early, pieces), out...  53.9 us
    pallas_call x1, Pallas kernels, packed_tiles(): pl.pallas_call(functools.partial(gradient_kernel, span, early), out_shape...  7.8 us
    pallas_call x1, Pallas kernels, four_owners(): pl.pallas_call(functools.partial(choice_kernel, sizes), out_shape=jax.Sha...  1.3 us

commit v1 on v0

--- a/solution.py
+++ b/solution.py
@@ -294,7 +294,7 @@
             add([peer_twin], width)
         else:
             t3(peer_twin, p).wait_recv()
-            add([peer, peer_twin], column_tile)
+            add([peer, peer_twin], min(512, width) if p else column_tile)
         whole = part[here].astype(jnp.bfloat16)
         summed[here] = whole
         error = (
@@ -552,7 +552,7 @@
     in_smem = pl.BlockSpec(memory_space=pltpu.SMEM)
     choice = pl.pallas_call(
         functools.partial(choice_kernel, sizes),
-        out_shape=jax.ShapeDtypeStruct((1,), jnp.int32),
+        out_shape=pltpu.SMEM((1,), jnp.int32),
         in_specs=[in_smem],
         out_specs=in_smem,
         name="choice",

time: 64.1 us -> 62.9 us (0.981)
  between operations: 1.47 us -> 0.82 us
where the time goes in v1:
time: 62.9 us; the launch traced here: 63.7 us
  Pallas kernels  62.5 us (99%)
  between operations  0.82 us (1%)
    pallas_call x1, Pallas kernels, packed_tiles(): pl.pallas_call(functools.partial(gather_kernel, sent, early, pieces), out...  53.9 us
    pallas_call x1, Pallas kernels, packed_tiles(): pl.pallas_call(functools.partial(gradient_kernel, span, early), out_shape...  7.8 us

profile of v1, /device:TPU:0, one launch (start us, length us, event | category | flops | bytes accessed | tf_op | source)
XLA Modules:
  0.0 63.7 jit_solution(2048541688691977719)
XLA Ops:
  0.6 0.8 %choice.1 = s32[1]{0:T(128)S(4)} custom-call(s32[32]{0:T(128)} %live_ref.1), custom_call_target="tpu_custom_call" | custom-call | tf_op jit(solution)/shard_map/choice/pallas_call | solution.py:553
  1.4 62.1 %conditional.1 = ((f32[640,1024]{1,0:T(8,128)}, f32[4,1024,1024]{2,1,0:T(8,128)})) conditional(s32[]{:T(128)} %bitcast.20, (bf16[160,4096]{1,0:T(8,128)(2,1)}, f32[1024]{0:T(1024)}, f32[1024]{0:T(1024)}, bf16[640,1024]{1,0:T(8,128)(2,1)}, s32[32]{0:T(128)}, /*index=5*/bf16[4096,1024]{1,0:T(8,128)(2,1)}, ...), branch_computations={%region_0.0_spmd, %region_1.0_spmd, %region_2.0_spmd, %region_3.0_... | conditional | bytes 16960 | solution.py:560
  1.4 0.0 copy-start.1
  1.5 0.0 copy-start.6
  1.5 53.9 %gather_codes_32_9.1 = (bf16[4,512,1024]{2,1,0:T(8,128)(2,1)S(1)}, bf16[512,1024]{1,0:T(8,128)(2,1)S(1)}, bf16[512,1024]{1,0:T(8,128)(2,1)S(1)}) custom-call(bf16[10,16,4096]{2,1,0:T(8,128)(2,1)} %bitcast.22, s32[32]{0:T(128)} %get-tuple-element.80.live_hbm.live_ref, bf16[4096,1024]{1,0:T(8,128)(2,1)} %get-tuple-element.82.enc_hbm, f32[1,1024]{1,0:T(1,128)} %bitcast.42, ...), custom_call_target="tpu_custom_call" | custom-call | tf_op jit(solution)/shard_map/cond/branch_1_fun/gather_codes_32_9/pallas_call | solution.py:473
  55.4 0.0 copy-done.1
  55.4 0.0 copy-done.6
  55.4 7.8 %gradient_32_9.1 = (f32[640,1024]{1,0:T(8,128)}, f32[4,1024,1024]{2,1,0:T(8,128)}) custom-call(s32[32]{0:T(128)S(1)} %copy-done.6, bf16[4,512,1024]{2,1,0:T(8,128)(2,1)S(1)} %get-tuple-element.87.codes_ref, bf16[512,1024]{1,0:T(8,128)(2,1)S(1)} %get-tuple-element.88.residual_ref, bf16[512,1024]{1,0:T(8,128)(2,1)S(1)} %get-tuple-element.89.summed_ref, ...), custom_call_target="tpu_custom_call" | custom-call | tf_op jit(solution)/shard_map/cond/branch_1_fun/gradient_32_9/pallas_call | solution.py:525
Async XLA Ops:
  1.4 54.0 %copy-start.1 = (f32[1024]{0:T(1024)S(1)}, f32[1024]{0:T(1024)}, u32[]{:S(2)}) copy-start(f32[1024]{0:T(1024)} %get-tuple-element.85) | copy-start | bytes 12292 | tf_op jit(solution)/shard_map/cond
  1.5 54.0 %copy-start.6 = (s32[32]{0:T(128)S(1)}, s32[32]{0:T(128)}, u32[]{:S(2)}) copy-start(s32[32]{0:T(128)} %get-tuple-element.80.live_hbm.live_ref) | copy-start | bytes 388 | tf_op jit(solution)/shard_map/cond

commit v2 on v1

--- a/solution.py
+++ b/solution.py
@@ -294,7 +294,7 @@
             add([peer_twin], width)
         else:
             t3(peer_twin, p).wait_recv()
-            add([peer, peer_twin], min(512, width) if p else column_tile)
+            add([peer, peer_twin], width if p else column_tile)
         whole = part[here].astype(jnp.bfloat16)
         summed[here] = whole
         error = (

time: 62.9 us -> 66.8 us (1.062); the launches traced: 63.7 us -> 66.6 us
  Pallas kernels: 62.5 us -> 65.3 us
    pallas_call x1, Pallas kernels: 53.9 us -> 56.8 us  [packed_tiles(): pl.pallas_call(functools.partial(gather_kernel, sent, early, pieces), out...]
where the time goes in v2:
time: 66.8 us; the launch traced here: 66.6 us
  Pallas kernels  65.3 us (98%)
  between operations  0.82 us (1%)
    pallas_call x1, Pallas kernels, packed_tiles(): pl.pallas_call(functools.partial(gather_kernel, sent, early, pieces), out...  56.8 us
    pallas_call x1, Pallas kernels, packed_tiles(): pl.pallas_call(functools.partial(gradient_kernel, span, early), out_shape...  7.8 us

profile of v2, /device:TPU:0, one launch (start us, length us, event | category | flops | bytes accessed | tf_op | source)
XLA Modules:
  0.0 66.6 jit_solution(3407340999190899828)
XLA Ops:
  0.6 0.8 %choice.1 = s32[1]{0:T(128)S(4)} custom-call(s32[32]{0:T(128)} %live_ref.1), custom_call_target="tpu_custom_call" | custom-call | tf_op jit(solution)/shard_map/choice/pallas_call | solution.py:553
  1.4 65.0 %conditional.1 = ((f32[640,1024]{1,0:T(8,128)}, f32[4,1024,1024]{2,1,0:T(8,128)})) conditional(s32[]{:T(128)} %bitcast.20, (bf16[160,4096]{1,0:T(8,128)(2,1)}, f32[1024]{0:T(1024)}, f32[1024]{0:T(1024)}, bf16[640,1024]{1,0:T(8,128)(2,1)}, s32[32]{0:T(128)}, /*index=5*/bf16[4096,1024]{1,0:T(8,128)(2,1)}, ...), branch_computations={%region_0.0_spmd, %region_1.0_spmd, %region_2.0_spmd, %region_3.0_... | conditional | bytes 16960 | solution.py:560
  1.6 0.0 copy-start.2
  1.6 0.0 copy-start.7
  1.7 56.8 %gather_codes_32_10.1 = (bf16[4,512,1024]{2,1,0:T(8,128)(2,1)S(1)}, bf16[512,1024]{1,0:T(8,128)(2,1)S(1)}, bf16[512,1024]{1,0:T(8,128)(2,1)S(1)}) custom-call(bf16[10,16,4096]{2,1,0:T(8,128)(2,1)} %bitcast.23, s32[32]{0:T(128)} %get-tuple-element.90.live_hbm.live_ref, bf16[4096,1024]{1,0:T(8,128)(2,1)} %get-tuple-element.92.enc_hbm, f32[1,1024]{1,0:T(1,128)} %bitcast.43, ...), custom_call_target="tpu_custom_call" | custom-call | tf_op jit(solution)/shard_map/cond/branch_2_fun/gather_codes_32_10/pallas_call | solution.py:473
  58.4 0.0 copy-done.2
  58.4 0.0 copy-done.7
  58.4 7.8 %gradient_32_10.1 = (f32[640,1024]{1,0:T(8,128)}, f32[4,1024,1024]{2,1,0:T(8,128)}) custom-call(s32[32]{0:T(128)S(1)} %copy-done.7, bf16[4,512,1024]{2,1,0:T(8,128)(2,1)S(1)} %get-tuple-element.97.codes_ref, bf16[512,1024]{1,0:T(8,128)(2,1)S(1)} %get-tuple-element.98.residual_ref, bf16[512,1024]{1,0:T(8,128)(2,1)S(1)} %get-tuple-element.99.summed_ref, ...), custom_call_target="tpu_custom_call" | custom-call | tf_op jit(solution)/shard_map/cond/branch_2_fun/gradient_32_10/pallas_call | solution.py:525
Async XLA Ops:
  1.6 56.8 %copy-start.2 = (f32[1024]{0:T(1024)S(1)}, f32[1024]{0:T(1024)}, u32[]{:S(2)}) copy-start(f32[1024]{0:T(1024)} %get-tuple-element.95) | copy-start | bytes 12292 | tf_op jit(solution)/shard_map/cond
  1.6 56.8 %copy-start.7 = (s32[32]{0:T(128)S(1)}, s32[32]{0:T(128)}, u32[]{:S(2)}) copy-start(s32[32]{0:T(128)} %get-tuple-element.90.live_hbm.live_ref) | copy-start | bytes 388 | tf_op jit(solution)/shard_map/cond
